TPU v7x, 512 devices: a whole 4x4x16 slice. The times are simulated.
512 devices in a mesh: rep: 4 (over y), own: 128 (over x, z, core).
Axes of the slice: x: 4, y: 4, z: 16, core: 2. Of those that a mesh axis runs over, the one named last changes fastest.
Arguments:
- local_weights: bfloat16 [4, 192, 384, 768], P('rep', None, 'own'), may hold values from -6 to 6
- anchor: float32 [256, 384, 768], P('own', 'rep'), may hold values from -6 to 6
- momentum: float32 [256, 384, 768], P('own', 'rep'), may hold values from -6 to 6
- owners: int32 [192], replicated, may hold values from 0 to 127, as said below
Outputs:
- new_weights: float32 [192, 384, 768], P(None, 'own')
- new_momentum: float32 [256, 384, 768], P('own', 'rep')
Inputs may be any that keep to these rules, and one draw needn't show every extreme that they name: Blocks 2i and 2i+1 for i < 48 form one attention projection and have the same owner; different projections have different owners; the 96 embedding blocks that follow go to the owners holding no projection, in runs of consecutive blocks; every owner holds at least one block and at most 2, and some owner holds exactly 2.
All inputs are finite; a program needn't handle non-finite values.
Results may differ from a plain program's by a relative error of at most 0.0003.
Values may be sent and summed in bfloat16 or wider, within the bound.
A program may use at most 64 MiB of HBM per device.

v0:
```python
import jax
import jax.numpy as jnp
from jax import lax
from jax.sharding import PartitionSpec as P

outer_rate = 0.7
momentum_rate = 0.9


def local(local_weights, anchor, momentum, owners):
    n_own = lax.axis_size("own")
    n_rep = lax.axis_size("rep")
    blocks = owners.shape[0]
    stripe = local_weights.shape[2]
    width = local_weights.shape[3]
    slots = anchor.shape[0]
    block_rows = stripe * n_own
    index = jnp.arange(blocks, dtype=jnp.int32)
    same = (owners[None, :] == owners[:, None]) & (index[None, :] < index[:, None])
    slot = jnp.sum(same.astype(jnp.int32), axis=1)
    place = owners * slots + slot
    targets = jnp.arange(n_own * slots, dtype=jnp.int32)
    picker = targets[:, None] == place[None, :]
    source = jnp.sum(jnp.where(picker, index[None, :], 0), axis=1)
    valid = jnp.any(picker, axis=1)
    mine = lax.axis_index("own") * slots + jnp.arange(slots, dtype=jnp.int32)
    live = jnp.any(mine[:, None] == place[None, :], axis=1)
    rows_here = local_weights[0]
    flat = rows_here.reshape(blocks, stripe * width)
    outgoing = jnp.where(
        valid[:, None], jnp.take(flat, source, axis=0), jnp.zeros((), jnp.bfloat16)
    )
    outgoing = outgoing.reshape(n_own, slots, stripe, width)
    arrived = lax.all_to_all(outgoing, "own", split_axis=0, concat_axis=2, tiled=True)
    arrived = arrived.reshape(slots, block_rows, width).astype(jnp.float32)
    total = lax.psum_scatter(arrived, "rep", scatter_dimension=1, tiled=True)
    mean_local = total / n_rep
    outer_grad = anchor - mean_local
    moment = momentum_rate * momentum + outer_grad
    updated = anchor - outer_rate * (outer_grad + momentum_rate * moment)
    alive = live[:, None, None]
    new_momentum = jnp.where(alive, moment, 0.0)
    updated = jnp.where(alive, updated, 0.0)
    whole = lax.all_gather(updated, "rep", axis=1, tiled=True)
    whole = whole.reshape(slots, n_own, stripe, width)
    returned = lax.all_to_all(whole, "own", split_axis=1, concat_axis=0, tiled=True)
    returned = returned.reshape(n_own * slots, stripe * width)
    new_weights = jnp.take(returned, place, axis=0)
    new_weights = new_weights.reshape(blocks, stripe, width)
    return (new_weights, new_momentum)


def solution(mesh):
    return jax.shard_map(
        local,
        mesh=mesh,
        in_specs=(P("rep", None, "own", None), P("own", "rep", None), P("own", "rep", None), P()),
        out_specs=(P(None, "own", None), P("own", "rep", None)),
        check_vma=False,
    )
```

profile of v0, /device:TPU:1, one launch (start us, length us, event | category | flops | bytes accessed | tf_op | source)
XLA Modules:
  0.0 356.4 jit_solution(2367220810949827903)
XLA Ops:
  7.2 0.9 convert_reduce_fusion
  8.1 0.7 compare_and_fusion.1
  9.2 1.9 copy.26
  11.3 1.4 gather_fusion
  12.7 0.6 gather.13
  13.3 0.2 broadcast_in_dim.77
  13.5 1.3 select_select_fusion
  14.8 1.0 copy.27
  15.8 79.9 %all_to_all.24 = bf16[128,2,3,768]{3,1,2,0:T(2,128)(2,1)S(1)} all-to-all(bf16[128,2,3,768]{3,1,2,0:T(2,128)(2,1)S(1)} %copy.27), channel_id=1, replica_groups=mesh['rep'=4,'own'=128] {'own'}, dimensions={0} | all-to-all | bytes 2359296 | tf_op jit(solution)/shard_map/all_to_all | solution.py:34
  95.8 2.2 bitcast_convert_fusion
  98.0 1.3 dynamic-slice
  100.1 0.2 compare_reduce_fusion
  100.2 69.7 %all-reduce.3.cloned.1.call-done = f32[2,384,768]{2,0,1:T(2,128)} async-done(((f32[2,384,768]{2,0,1:T(2,128)}), f32[2,384,768]{2,0,1:T(2,128)}) %all-reduce.3.cloned.1.call-update) | async-done | bytes 2359312
  170.0 3.3 broadcast_select_fusion.1
  173.3 40.7 %all-gather.2.cloned.1.call-done = f32[2,384,768]{2,0,1:T(2,128)} async-done(((f32[2,96,768]{2,0,1:T(2,128)}), f32[2,384,768]{2,0,1:T(2,128)}) %all-gather.2.cloned.1.call-update) | async-done | bytes 2359312 | tf_op jit(solution)/shard_map/all_gather | solution.py:44
  214.0 16.8 %all-to-all-start.1 = ((f32[2,128,3,768]{3,0,2,1:T(2,128)}), f32[2,128,3,768]{3,0,2,1:T(2,128)S(1)}, u32[]{:S(2)}, u32[]{:S(2)}) async-start(f32[2,128,3,768]{3,0,2,1:T(2,128)} %bitcast.26), calls=%async_computation.1 | async-start | bytes 4718592 | tf_op jit(solution)/shard_map/all_to_all | solution.py:46
  230.8 0.9 copy.33
  231.7 109.2 %all-to-all-done.1 = f32[2,128,3,768]{3,0,2,1:T(2,128)S(1)} async-done(((f32[2,128,3,768]{3,0,2,1:T(2,128)}), f32[2,128,3,768]{3,0,2,1:T(2,128)S(1)}, u32[]{:S(2)}, u32[]{:S(2)}) %all-to-all-start.1) | async-done | bytes 2359328 | tf_op jit(solution)/shard_map/all_to_all | solution.py:46
  340.9 0.8 copy.31
  341.7 0.4 copy.35
  342.1 2.5 gather_fusion.1
  344.6 2.8 gather.15
  347.4 0.6 broadcast_select_fusion
  348.0 1.5 copy.32
  (18 shorter events, 0.6 us)
Async XLA Ops:
  7.2 162.8 %all-reduce.3.cloned.1.call-start = ((), (), s32[]{:S(2)}) async-start(), calls=%async_computation.3 | async-start | bytes 4718592
  98.0 72.0 %copy-start = (f32[2,96,768]{2,1,0:T(8,128)S(1)}, f32[2,96,768]{2,1,0:T(8,128)}, u32[]{:S(2)}) copy-start(f32[2,96,768]{2,1,0:T(8,128)} %param.6) | copy-start | bytes 1769476
  98.0 72.0 %copy-start.1 = (f32[2,96,768]{2,1,0:T(8,128)S(1)}, f32[2,96,768]{2,1,0:T(8,128)}, u32[]{:S(2)}) copy-start(f32[2,96,768]{2,1,0:T(8,128)} %param.5) | copy-start | bytes 1769476
  98.0 116.0 %all-gather.2.cloned.1.call-start = ((), (), s32[]{:S(2)}) async-start(), calls=%async_computation.2 | async-start | bytes 2949120 | tf_op jit(solution)/shard_map/all_gather | solution.py:44
  214.0 126.9 %all-to-all-start.1 = ((f32[2,128,3,768]{3,0,2,1:T(2,128)}), f32[2,128,3,768]{3,0,2,1:T(2,128)S(1)}, u32[]{:S(2)}, u32[]{:S(2)}) async-start(f32[2,128,3,768]{3,0,2,1:T(2,128)} %bitcast.26), calls=%async_computation.1 | async-start | bytes 4718592 | tf_op jit(solution)/shard_map/all_to_all | solution.py:46
Sparse Core Ops, SparseCore 0:
  98.1 71.8 all-reduce.2
  173.5 40.4 all-gather.1
where the time goes:
time: 357 us; the launch traced here: 356 us
  waiting for transfers between devices  220 us (62%)
  blocking collectives  79.9 us (22%)
  starting transfers between devices  16.9 us (5%)
  local copies, waits for them, and re-layouts  15.6 us (4%)
  between operations  14.8 us (4%)
  other arithmetic  9.54 us (3%)
    all_to_all x1, waiting for transfers between devices, local(): lax.all_to_all(whole, 'own', split_axis=1, concat_axis=0, tiled=True)  109 us
    all_to_all x1, blocking collectives, local(): lax.all_to_all(outgoing, 'own', split_axis=0, concat_axis=2, tiled=True)  79.9 us
    unnamed x3, waiting for transfers between devices  69.8 us
    all_gather x1, waiting for transfers between devices, local(): whole = lax.all_gather(updated, 'rep', axis=1, tiled=True)  40.7 us
    all_to_all x1, starting transfers between devices, local(): lax.all_to_all(whole, 'own', split_axis=1, concat_axis=0, tiled=True)  16.8 us
  transfers between devices with their start and end apart: 3, of which 3 were waited for; matrix products, arithmetic and copies ran while one was open for 1% of the time, Pallas kernels for 0%

commit v1 on v0

--- a/solution.py
+++ b/solution.py
@@ -41,7 +41,15 @@
     alive = live[:, None, None]
     new_momentum = jnp.where(alive, moment, 0.0)
     updated = jnp.where(alive, updated, 0.0)
-    whole = lax.all_gather(updated, "rep", axis=1, tiled=True)
+    whole = jnp.concatenate(
+        lax.all_to_all(
+            jnp.stack([updated] * lax.axis_size("rep"), 0),
+            axis_name="rep",
+            split_axis=0,
+            concat_axis=0,
+        ),
+        1,
+    )
     whole = whole.reshape(slots, n_own, stripe, width)
     returned = lax.all_to_all(whole, "own", split_axis=1, concat_axis=0, tiled=True)
     returned = returned.reshape(n_own * slots, stripe * width)

time: 357 us -> 348 us (0.975)
  waiting for transfers between devices: 220 us -> 179 us
  blocking collectives: 79.9 us -> 111 us
    all_gather x1 -> x0, waiting for transfers between devices: 40.7 us -> none  [local(): whole = lax.all_gather(updated, 'rep', axis=1, tiled=True)]
    all_to_all x0 -> x1, blocking collectives: none -> 31.4 us  [local(): lax.all_to_all(jnp.stack([updated] * lax.axis_size('rep'), 0), axis_name=...]
    unnamed x3 -> x2, waiting for transfers between devices: 69.8 us -> 69.8 us
  transfers between devices with their start and end apart: 3 -> 2, of which waited for: 3 -> 2; matrix products, arithmetic and copies ran while one was open for 1% -> 1% of each run, Pallas kernels for 0% -> 0%
where the time goes in v1:
time: 348 us
  waiting for transfers between devices  179 us (51%)
  blocking collectives  111 us (32%)
  starting transfers between devices  17.9 us (5%)
  local copies, waits for them, and re-layouts  16.2 us (5%)
  between operations  14.8 us (4%)
  other arithmetic  8.72 us (3%)
    all_to_all x1, waiting for transfers between devices, local(): lax.all_to_all(whole, 'own', split_axis=1, concat_axis=0, tiled=True)  109 us
    all_to_all x1, blocking collectives, local(): lax.all_to_all(outgoing, 'own', split_axis=0, concat_axis=2, tiled=True)  79.9 us
    unnamed x2, waiting for transfers between devices  69.8 us
    all_to_all x1, blocking collectives, local(): lax.all_to_all(jnp.stack([updated] * lax.axis_size('rep'), 0), axis_name=...  31.4 us
    all_to_all x1, starting transfers between devices, local(): lax.all_to_all(whole, 'own', split_axis=1, concat_axis=0, tiled=True)  17.9 us
  transfers between devices with their start and end apart: 2, of which 2 were waited for; matrix products, arithmetic and copies ran while one was open for 1% of the time, Pallas kernels for 0%

profile of v1, /device:TPU:1, one launch (start us, length us, event | category | flops | bytes accessed | tf_op | source)
XLA Modules:
  0.0 348.0 jit_solution(1530592718284688268)
XLA Ops:
  7.2 0.9 convert_reduce_fusion
  8.1 0.7 compare_and_fusion.1
  9.2 1.9 copy.25
  11.3 1.4 gather_fusion
  12.7 0.6 gather.13
  13.5 1.3 select_select_fusion
  14.8 1.0 copy.26
  15.8 79.9 %all_to_all.29 = bf16[128,2,3,768]{3,1,2,0:T(2,128)(2,1)S(1)} all-to-all(bf16[128,2,3,768]{3,1,2,0:T(2,128)(2,1)S(1)} %copy.26), channel_id=1, replica_groups=mesh['rep'=4,'own'=128] {'own'}, dimensions={0} | all-to-all | bytes 2359296 | tf_op jit(solution)/shard_map/all_to_all | solution.py:34
  95.8 2.2 bitcast_convert_fusion
  98.0 1.4 dynamic-slice
  100.0 0.2 compare_reduce_fusion
  100.2 69.8 %all-reduce.3.cloned.1.call-done = f32[2,384,768]{2,0,1:T(2,128)} async-done(((f32[2,384,768]{2,0,1:T(2,128)}), f32[2,384,768]{2,0,1:T(2,128)}) %all-reduce.3.cloned.1.call-update) | async-done | bytes 2359312
  170.0 2.5 broadcast_select_fusion.1
  172.5 0.6 stack.2
  173.1 31.4 %all_to_all.30 = f32[4,2,96,768]{3,1,2,0:T(2,128)} all-to-all(f32[4,2,96,768]{3,1,2,0:T(2,128)S(1)} %stack.2), channel_id=1, replica_groups=mesh['rep'=4,'own'=128] {'rep'}, dimensions={0} | all-to-all | bytes 4718592 | tf_op jit(solution)/shard_map/all_to_all | solution.py:45
  204.5 17.9 %all-to-all-start.2 = ((f32[2,128,3,768]{3,0,2,1:T(2,128)}), f32[2,128,3,768]{3,0,2,1:T(2,128)S(1)}, u32[]{:S(2)}, u32[]{:S(2)}) async-start(f32[2,128,3,768]{3,0,2,1:T(2,128)} %bitcast.7), calls=%async_computation.2 | async-start | bytes 4718592 | tf_op jit(solution)/shard_map/all_to_all | solution.py:54
  222.4 0.9 copy.32
  223.3 109.2 %all-to-all-done.2 = f32[2,128,3,768]{3,0,2,1:T(2,128)S(1)} async-done(((f32[2,128,3,768]{3,0,2,1:T(2,128)}), f32[2,128,3,768]{3,0,2,1:T(2,128)S(1)}, u32[]{:S(2)}, u32[]{:S(2)}) %all-to-all-start.2) | async-done | bytes 2359328 | tf_op jit(solution)/shard_map/all_to_all | solution.py:54
  332.5 0.8 copy.30
  333.3 0.4 copy.34
  333.7 2.5 gather_fusion.1
  336.2 2.8 gather.15
  339.0 0.6 broadcast_select_fusion
  339.6 1.5 copy.31
  (17 shorter events, 0.7 us)
Async XLA Ops:
  7.2 162.8 %all-reduce.3.cloned.1.call-start = ((), (), s32[]{:S(2)}) async-start(), calls=%async_computation.3 | async-start | bytes 4718592
  98.0 72.0 %copy-start = (f32[2,96,768]{2,1,0:T(8,128)S(1)}, f32[2,96,768]{2,1,0:T(8,128)}, u32[]{:S(2)}) copy-start(f32[2,96,768]{2,1,0:T(8,128)} %param.6) | copy-start | bytes 1769476
  98.0 72.0 %copy-start.1 = (f32[2,96,768]{2,1,0:T(8,128)S(1)}, f32[2,96,768]{2,1,0:T(8,128)}, u32[]{:S(2)}) copy-start(f32[2,96,768]{2,1,0:T(8,128)} %param.5) | copy-start | bytes 1769476
  204.5 127.9 %all-to-all-start.2 = ((f32[2,128,3,768]{3,0,2,1:T(2,128)}), f32[2,128,3,768]{3,0,2,1:T(2,128)S(1)}, u32[]{:S(2)}, u32[]{:S(2)}) async-start(f32[2,128,3,768]{3,0,2,1:T(2,128)} %bitcast.7), calls=%async_computation.2 | async-start | bytes 4718592 | tf_op jit(solution)/shard_map/all_to_all | solution.py:54
Sparse Core Ops, SparseCore 0:
  98.1 71.8 all-reduce.2
